TPU v7x, 512 devices: a whole 4x8x8 slice. The times are simulated.
512 devices in a mesh: rows: 32 (over z_lo, y), cols: 16 (over x, z_hi, core).
Axes of the slice: x: 4, y: 8, z: 8 (z_hi: 2, z_lo: 4; z = z_hi * 4 + z_lo), core: 2. Of those that a mesh axis runs over, the one named last changes fastest.
Arguments:
- series: float32 [2097152], P(('rows', 'cols')), may hold values from -6 to 6
- tile_list: int32 [3, 2048], P(None, 'rows'), may hold values from 0 to 4094, as said below
Outputs:
- profile: float32 [2097152], P(('rows', 'cols'))
Inputs may be any that keep to these rules, and one draw needn't show every extreme that they name: The columns of tile_list lying on one index of rows list 64 distinct tiles (row block, offset) of that row group: the row block lies in the group, the offset is below 8, and row block plus offset is at most 4094. Every group but the last lists a tile whose column block lies in the next group; the last group lists the tile of row block 4094 and offset 0. The third row is an index of cols; in each group no index owns more than 8 tiles and one owns exactly 8.
All inputs are finite; a program needn't handle non-finite values.
Results may differ from a plain program's by a relative error of at most 0.0001.
Values sent between devices are 32-bit elements; how exact they have to be, the bound alone decides.
A program may use at most 64 MiB of HBM per device.

v0:
```python
import math
import jax
import jax.numpy as jnp
from jax import lax
from jax.sharding import PartitionSpec as P

M = 256
B = 512
BPR = 128
CAP = 8
NEXT = 4096
EXCL = 64


def passed_along(block, axis, distance):
    devices = range(lax.axis_size(axis))
    route = [(i - distance, i) for i in devices if i - distance in devices]
    return lax.ppermute(block, axis, route)


def hankel(values, rows, width):
    length = values.shape[0]
    flat = jnp.concatenate([jnp.tile(values, rows), jnp.zeros((rows,), values.dtype)])
    return flat.reshape(rows, length + 1)[:, :width]


def normalize(values):
    windows = hankel(values, B, M)
    centre = windows - jnp.mean(windows, axis=1, keepdims=True)
    spread = jnp.mean(centre * centre, axis=1)
    factor = lax.rsqrt(spread + 1e-05) / math.sqrt(M)
    return centre * factor[:, None]


def tile_maxima(left_data, right_data, offset):
    left_z = normalize(left_data)
    right_z = normalize(right_data)
    corr = lax.dot_general(
        left_z,
        right_z,
        (((1,), (1,)), ((), ())),
        precision=lax.Precision.HIGHEST,
        preferred_element_type=jnp.float32,
    )
    row_pos = lax.broadcasted_iota(jnp.int32, (B, B), 0)
    col_pos = lax.broadcasted_iota(jnp.int32, (B, B), 1)
    keep = offset * B + col_pos - row_pos >= EXCL
    corr = jnp.where(keep, corr, jnp.float32(-1.0))
    return (jnp.max(corr, axis=1), jnp.max(corr, axis=0))


def raise_block(partial_max, start, values):
    current = lax.dynamic_slice_in_dim(partial_max, start, B)
    return lax.dynamic_update_slice_in_dim(partial_max, jnp.maximum(current, values), start, 0)


def on_device(series, tile_list):
    piece = series.shape[0]
    col_count = lax.axis_size("cols")
    seg_len = piece * col_count
    group = lax.axis_index("rows")
    col_id = lax.axis_index("cols")
    segment = lax.all_gather(series, "cols", axis=0, tiled=True)
    head = passed_along(segment[:NEXT], "rows", -1)
    signal = jnp.concatenate([segment, head])
    foreign = (tile_list[2] != col_id).astype(jnp.int32)
    order = jnp.argsort(foreign, stable=True)[:CAP]
    live = tile_list[2][order] == col_id
    slots = CAP
    partial_max = jnp.full((seg_len + NEXT,), -1.0, jnp.float32)

    def step(index, partial_max):
        which = order[index]
        local_block = tile_list[0, which] - group * BPR
        offset = tile_list[1, which]
        row_start = local_block * B
        col_start = (local_block + offset) * B
        left_data = lax.dynamic_slice_in_dim(signal, row_start, B + M)
        right_data = lax.dynamic_slice_in_dim(signal, col_start, B + M)
        row_max, col_max = tile_maxima(left_data, right_data, offset)
        active = live[index]
        row_max = jnp.where(active, row_max, jnp.float32(-1.0))
        col_max = jnp.where(active, col_max, jnp.float32(-1.0))
        partial_max = raise_block(partial_max, row_start, row_max)
        return raise_block(partial_max, col_start, col_max)

    partial_max = lax.fori_loop(0, slots, step, partial_max)
    own_part = partial_max[:seg_len]
    spill = partial_max[seg_len:]
    own_part, spill = lax.pmax((own_part, spill), "cols")
    arrived = passed_along(spill, "rows", 1)
    arrived = jnp.where(group > 0, arrived, jnp.float32(-1.0))
    own_part = jnp.concatenate([jnp.maximum(own_part[:NEXT], arrived), own_part[NEXT:]])
    return lax.dynamic_slice_in_dim(own_part, col_id * piece, piece)


def solution(mesh):
    in_specs = (P(("rows", "cols")), P(None, "rows"))
    out_specs = P(("rows", "cols"))
    return jax.shard_map(
        on_device, mesh=mesh, in_specs=in_specs, out_specs=out_specs, check_vma=False
    )
```

profile of v0, /device:TPU:1, one launch (start us, length us, event | category | flops | bytes accessed | tf_op | source)
XLA Modules:
  0.0 393.8 jit_solution(1997206631718759267)
XLA Ops:
  6.5 37.6 %all_gather.3 = f32[65536]{0:T(1024)S(1)} all-gather(f32[4096]{0:T(1024)} %param.4), channel_id=1, replica_groups=mesh['rows'=32,'cols'=16] {'cols'}, dimensions={0}, use_global_device_ids=true | all-gather | bytes 278528 | tf_op jit(solution)/shard_map/all_gather | solution.py:63
  46.8 2.0 sort.17
  50.3 152.8 %while.15 = (s32[]{:T(128)}, f32[69632]{0:T(1024)}, s32[8]{0:T(128)S(1)}, s32[3,64]{1,0:T(4,128)}, s32[]{:T(128)}, /*index=5*/pred[8]{0:T(512)(128)(4,1)S(1)}, f...) while((s32[]{:T(128)}, f32[69632]{0:T(1024)}, ...), condition=%wide.region_8.9_spmd, body=%wide.region_1.8_spmd.sunk | while | flops 808193536 | bytes 33783220 | solution.py:87
  61.9 2.4 fusion.12
  65.0 2.2 maximum_dynamic-update-slice_fusion.4
  67.2 2.2 maximum_dynamic-update-slice_fusion.5
  78.4 1.6 reshape.63
  81.0 2.4 fusion.12
  84.1 2.2 maximum_dynamic-update-slice_fusion.4
  86.3 2.2 maximum_dynamic-update-slice_fusion.5
  100.1 2.4 fusion.12
  103.1 2.2 maximum_dynamic-update-slice_fusion.4
  105.3 2.2 maximum_dynamic-update-slice_fusion.5
  119.2 2.4 fusion.12
  122.2 2.2 maximum_dynamic-update-slice_fusion.4
  124.4 2.2 maximum_dynamic-update-slice_fusion.5
  138.3 2.4 fusion.12
  141.3 2.2 maximum_dynamic-update-slice_fusion.4
  143.5 2.2 maximum_dynamic-update-slice_fusion.5
  157.4 2.4 fusion.12
  160.4 2.2 maximum_dynamic-update-slice_fusion.4
  162.6 2.2 maximum_dynamic-update-slice_fusion.5
  176.5 2.4 fusion.12
  179.5 2.2 maximum_dynamic-update-slice_fusion.4
  181.8 2.2 maximum_dynamic-update-slice_fusion.5
  195.6 2.4 fusion.12
  198.7 2.2 maximum_dynamic-update-slice_fusion.4
  200.9 2.2 maximum_dynamic-update-slice_fusion.5
  203.1 1.7 slice.43
  205.5 76.3 %pmax.15 = f32[4096]{0:T(1024)S(1)} all-reduce(f32[4096]{0:T(1024)S(1)} %slice.45), channel_id=1, replica_groups=mesh['rows'=32,'cols'=16] {'cols'}, use_global_device_ids=true, to_apply=%region_10.11 | all-reduce | flops 4096 | bytes 32768 | tf_op jit(solution)/shard_map/pmax | solution.py:90
  281.8 4.0 %collective-permute-start.1 = (f32[4096]{0:T(1024)S(1)}, f32[4096]{0:T(1024)S(1)}, u32[]{:S(2)}, u32[]{:S(2)}) collective-permute-start(f32[4096]{0:T(1024)S(1)} %pmax.15), channel_id=1, source_target_pairs={{0,16},{16,32},{32,48},{48,64},{64,80},{80,96},{96,112},{112,128},... | collective-permute-start | bytes 49160 | tf_op jit(solution)/shard_map/ppermute | solution.py:18
  285.8 98.8 %all-reduce.4.cloned.1.call-done = f32[65536]{0:T(1024)} async-done(((f32[65536]{0:T(1024)}), f32[65536]{0:T(1024)}) %all-reduce.4.cloned.1.call-update) | async-done | bytes 262160 | tf_op jit(solution)/shard_map/pmax | solution.py:90
  (226 shorter events, 71.7 us)
Async XLA Ops:
  6.5 378.1 %all-reduce.4.cloned.1.call-start = ((), (), s32[]{:S(2)}) async-start(), calls=%async_computation | async-start | bytes 524288 | tf_op jit(solution)/shard_map/pmax | solution.py:90
  44.1 5.4 %collective-permute-start = (f32[4096]{0:T(1024)S(1)}, f32[4096]{0:T(1024)S(1)}, u32[]{:S(2)}, u32[]{:S(2)}) collective-permute-start(f32[4096]{0:T(1024)S(1)} %slice.51), channel_id=1, source_target_pairs={{16,0},{32,16},{48,32},{64,48},{80,64},{96,80},{112,96},{128,112},... | collective-permute-start | bytes 49160 | tf_op jit(solution)/shard_map/ppermute | solution.py:18
  50.3 5.5 %copy-start.1 = (f32[69632]{0:T(1024)}, f32[69632]{0:T(1024)S(1)}, u32[]{:S(2)}) copy-start(f32[69632]{0:T(1024)S(1)} %get-tuple-element.293) | copy-start | bytes 835588 | tf_op jit(solution)/shard_map/while
  57.7 1.3 copy-start
  60.9 8.5 %copy-start.2 = (f32[69632]{0:T(1024)S(1)}, f32[69632]{0:T(1024)}, u32[]{:S(2)}) copy-start(f32[69632]{0:T(1024)} %copy-done.1) | copy-start | bytes 835588 | tf_op jit(solution)/shard_map/while
  69.4 5.5 %copy-start.1 = (f32[69632]{0:T(1024)}, f32[69632]{0:T(1024)S(1)}, u32[]{:S(2)}) copy-start(f32[69632]{0:T(1024)S(1)} %get-tuple-element.293) | copy-start | bytes 835588 | tf_op jit(solution)/shard_map/while
  76.8 1.3 copy-start
  80.0 8.5 %copy-start.2 = (f32[69632]{0:T(1024)S(1)}, f32[69632]{0:T(1024)}, u32[]{:S(2)}) copy-start(f32[69632]{0:T(1024)} %copy-done.1) | copy-start | bytes 835588 | tf_op jit(solution)/shard_map/while
  88.5 5.5 %copy-start.1 = (f32[69632]{0:T(1024)}, f32[69632]{0:T(1024)S(1)}, u32[]{:S(2)}) copy-start(f32[69632]{0:T(1024)S(1)} %get-tuple-element.293) | copy-start | bytes 835588 | tf_op jit(solution)/shard_map/while
  95.9 1.3 copy-start
  99.1 8.5 %copy-start.2 = (f32[69632]{0:T(1024)S(1)}, f32[69632]{0:T(1024)}, u32[]{:S(2)}) copy-start(f32[69632]{0:T(1024)} %copy-done.1) | copy-start | bytes 835588 | tf_op jit(solution)/shard_map/while
  107.5 5.5 %copy-start.1 = (f32[69632]{0:T(1024)}, f32[69632]{0:T(1024)S(1)}, u32[]{:S(2)}) copy-start(f32[69632]{0:T(1024)S(1)} %get-tuple-element.293) | copy-start | bytes 835588 | tf_op jit(solution)/shard_map/while
  115.0 1.3 copy-start
  118.2 8.5 %copy-start.2 = (f32[69632]{0:T(1024)S(1)}, f32[69632]{0:T(1024)}, u32[]{:S(2)}) copy-start(f32[69632]{0:T(1024)} %copy-done.1) | copy-start | bytes 835588 | tf_op jit(solution)/shard_map/while
  126.6 5.5 %copy-start.1 = (f32[69632]{0:T(1024)}, f32[69632]{0:T(1024)S(1)}, u32[]{:S(2)}) copy-start(f32[69632]{0:T(1024)S(1)} %get-tuple-element.293) | copy-start | bytes 835588 | tf_op jit(solution)/shard_map/while
  134.1 1.3 copy-start
  137.3 8.5 %copy-start.2 = (f32[69632]{0:T(1024)S(1)}, f32[69632]{0:T(1024)}, u32[]{:S(2)}) copy-start(f32[69632]{0:T(1024)} %copy-done.1) | copy-start | bytes 835588 | tf_op jit(solution)/shard_map/while
  145.8 5.5 %copy-start.1 = (f32[69632]{0:T(1024)}, f32[69632]{0:T(1024)S(1)}, u32[]{:S(2)}) copy-start(f32[69632]{0:T(1024)S(1)} %get-tuple-element.293) | copy-start | bytes 835588 | tf_op jit(solution)/shard_map/while
  153.2 1.3 copy-start
  156.4 8.5 %copy-start.2 = (f32[69632]{0:T(1024)S(1)}, f32[69632]{0:T(1024)}, u32[]{:S(2)}) copy-start(f32[69632]{0:T(1024)} %copy-done.1) | copy-start | bytes 835588 | tf_op jit(solution)/shard_map/while
  164.8 5.5 %copy-start.1 = (f32[69632]{0:T(1024)}, f32[69632]{0:T(1024)S(1)}, u32[]{:S(2)}) copy-start(f32[69632]{0:T(1024)S(1)} %get-tuple-element.293) | copy-start | bytes 835588 | tf_op jit(solution)/shard_map/while
  172.3 1.3 copy-start
  175.5 8.5 %copy-start.2 = (f32[69632]{0:T(1024)S(1)}, f32[69632]{0:T(1024)}, u32[]{:S(2)}) copy-start(f32[69632]{0:T(1024)} %copy-done.1) | copy-start | bytes 835588 | tf_op jit(solution)/shard_map/while
  184.0 5.5 %copy-start.1 = (f32[69632]{0:T(1024)}, f32[69632]{0:T(1024)S(1)}, u32[]{:S(2)}) copy-start(f32[69632]{0:T(1024)S(1)} %get-tuple-element.293) | copy-start | bytes 835588 | tf_op jit(solution)/shard_map/while
  191.4 1.3 copy-start
  194.6 8.5 %copy-start.2 = (f32[69632]{0:T(1024)S(1)}, f32[69632]{0:T(1024)}, u32[]{:S(2)}) copy-start(f32[69632]{0:T(1024)} %copy-done.1) | copy-start | bytes 835588 | tf_op jit(solution)/shard_map/while
  281.8 103.8 %collective-permute-start.1 = (f32[4096]{0:T(1024)S(1)}, f32[4096]{0:T(1024)S(1)}, u32[]{:S(2)}, u32[]{:S(2)}) collective-permute-start(f32[4096]{0:T(1024)S(1)} %pmax.15), channel_id=1, source_target_pairs={{0,16},{16,32},{32,48},{48,64},{64,80},{80,96},{96,112},{112,128},... | collective-permute-start | bytes 49160 | tf_op jit(solution)/shard_map/ppermute | solution.py:18
Sparse Core Ops, SparseCore 0:
  204.9 179.7 all-reduce.3
where the time goes:
time: 397 us; the launch traced here: 394 us
  blocking collectives  114 us (29%)
  waiting for transfers between devices  98.9 us (25%)
  local copies, waits for them, and re-layouts  65.3 us (16%)
  other arithmetic  45.5 us (11%)
  loops' own time  32.2 us (8%)
  matrix products  19.2 us (5%)
  between operations  13.5 us (3%)
  starting transfers between devices  5.3 us (1%)
    pmax x1, waiting for transfers between devices, on_device(): own_part, spill = lax.pmax((own_part, spill), 'cols')  98.8 us
    pmax x1, blocking collectives, on_device(): own_part, spill = lax.pmax((own_part, spill), 'cols')  76.3 us
    all_gather x1, blocking collectives, on_device(): segment = lax.all_gather(series, 'cols', axis=0, tiled=True)  37.6 us
    dynamic_update_slice x16, other arithmetic, raise_block(): lax.dynamic_update_slice_in_dim(partial_max, jnp.maximum(current, values)...  35.3 us
    another operation x1, loops' own time, on_device(): partial_max = lax.fori_loop(0, slots, step, partial_max)  32.2 us
    reshape x16, local copies, waits for them, and re-layouts, hankel(): return flat.reshape(rows, length + 1)[:, :width]  25.1 us
    dot_general x8, matrix products, tile_maxima(): lax.dot_general(left_z, right_z, (((1,), (1,)), ((), ())), precision=lax....  19.2 us
    dynamic_slice x8, local copies, waits for them, and re-layouts, step(): offset = tile_list[1, which]  11.4 us
  transfers between devices with their start and end apart: 3, of which 1 were waited for; matrix products, arithmetic and copies ran while one was open for 1% of the time, Pallas kernels for 0%

commit v1 on v0

--- a/solution.py
+++ b/solution.py
@@ -60,7 +60,9 @@
     seg_len = piece * col_count
     group = lax.axis_index("rows")
     col_id = lax.axis_index("cols")
-    segment = lax.all_gather(series, "cols", axis=0, tiled=True)
+    segment = jnp.concatenate(
+        lax.all_to_all(jnp.stack([series] * lax.axis_size("cols")), "cols", 0, 0), axis=0
+    )
     head = passed_along(segment[:NEXT], "rows", -1)
     signal = jnp.concatenate([segment, head])
     foreign = (tile_list[2] != col_id).astype(jnp.int32)

time: 397 us -> 382 us (0.962)
  blocking collectives: 114 us -> 78.1 us
  starting transfers between devices: 5.3 us -> 18.8 us
  waiting for transfers between devices: 98.9 us -> 111 us
  local copies, waits for them, and re-layouts: 65.3 us -> 60.9 us
    all_gather x1 -> x0, blocking collectives: 37.6 us -> none  [on_device(): segment = lax.all_gather(series, 'cols', axis=0, tiled=True)]
    all_to_all x0 -> x1, starting transfers between devices: none -> 14.3 us  [on_device(): lax.all_to_all(jnp.stack([series] * lax.axis_size('cols')), 'cols', 0, 0)]
    all_to_all x0 -> x1, waiting for transfers between devices: none -> 7.01 us  [on_device(): lax.all_to_all(jnp.stack([series] * lax.axis_size('cols')), 'cols', 0, 0)]
    dynamic_slice x8, local copies, waits for them, and re-layouts: 11.4 us -> 5.36 us  [step(): offset = tile_list[1, which]]
  transfers between devices with their start and end apart: 3 -> 4, of which waited for: 1 -> 3; matrix products, arithmetic and copies ran while one was open for 1% -> 2% of each run, Pallas kernels for 0% -> 0%
where the time goes in v1:
time: 382 us; the launch traced here: 379 us
  waiting for transfers between devices  111 us (29%)
  blocking collectives  78.1 us (20%)
  local copies, waits for them, and re-layouts  60.9 us (16%)
  other arithmetic  45.5 us (12%)
  loops' own time  32.2 us (8%)
  matrix products  19.3 us (5%)
  starting transfers between devices  18.8 us (5%)
  between operations  13.5 us (4%)
    pmax x1, waiting for transfers between devices, on_device(): own_part, spill = lax.pmax((own_part, spill), 'cols')  101 us
    pmax x1, blocking collectives, on_device(): own_part, spill = lax.pmax((own_part, spill), 'cols')  78.1 us
    dynamic_update_slice x16, other arithmetic, raise_block(): lax.dynamic_update_slice_in_dim(partial_max, jnp.maximum(current, values)...  35.3 us
    another operation x1, loops' own time, on_device(): partial_max = lax.fori_loop(0, slots, step, partial_max)  32.2 us
    reshape x16, local copies, waits for them, and re-layouts, hankel(): return flat.reshape(rows, length + 1)[:, :width]  25.1 us
    dot_general x8, matrix products, tile_maxima(): lax.dot_general(left_z, right_z, (((1,), (1,)), ((), ())), precision=lax....  19.3 us
    all_to_all x1, starting transfers between devices, on_device(): lax.all_to_all(jnp.stack([series] * lax.axis_size('cols')), 'cols', 0, 0)  14.3 us
  transfers between devices with their start and end apart: 4, of which 3 were waited for; matrix products, arithmetic and copies ran while one was open for 2% of the time, Pallas kernels for 0%

profile of v1, /device:TPU:1, one launch (start us, length us, event | category | flops | bytes accessed | tf_op | source)
XLA Modules:
  0.0 379.2 jit_solution(2330170746658820155)
XLA Ops:
  8.2 14.3 %all-to-all-start = ((f32[16,1,4096]{2,1,0:T(1,128)}), f32[16,1,4096]{2,1,0:T(1,128)S(1)}, u32[]{:S(2)}, u32[]{:S(2)}) async-start(f32[16,1,4096]{2,1,0:T(1,128)} %stack.2), calls=%async_computation | async-start | bytes 524288 | tf_op jit(solution)/shard_map/all_to_all | solution.py:64
  23.2 2.0 sort.17
  26.5 7.0 %all-to-all-done = f32[16,1,4096]{2,1,0:T(1,128)S(1)} async-done(((f32[16,1,4096]{2,1,0:T(1,128)}), f32[16,1,4096]{2,1,0:T(1,128)S(1)}, u32[]{:S(2)}, u32[]{:S(2)}) %all-to-all-start) | async-done | bytes 262176 | tf_op jit(solution)/shard_map/all_to_all | solution.py:64
  34.9 3.2 collective-permute-done
  38.8 146.8 %while.15 = (s32[]{:T(128)}, f32[69632]{0:T(1024)}, s32[8]{0:T(128)S(1)}, s32[3,64]{1,0:T(4,128)S(1)}, s32[]{:T(128)}, /*index=5*/pred[8]{0:T(512)(128)(4,1)S(1)...) while((s32[]{:T(128)}, f32[69632]{0:T(1024)}, ...), condition=%wide.region_8.9_spmd, body=%wide.region_1.8_spmd.sunk | while | flops 808193536 | bytes 33783220 | solution.py:89
  49.7 2.4 fusion.12
  52.7 2.2 maximum_dynamic-update-slice_fusion.4
  55.0 2.2 maximum_dynamic-update-slice_fusion.5
  68.0 2.4 fusion.12
  71.1 2.2 maximum_dynamic-update-slice_fusion.4
  73.3 2.2 maximum_dynamic-update-slice_fusion.5
  86.4 2.4 fusion.12
  89.4 2.2 maximum_dynamic-update-slice_fusion.4
  91.6 2.2 maximum_dynamic-update-slice_fusion.5
  104.7 2.4 fusion.12
  107.8 2.2 maximum_dynamic-update-slice_fusion.4
  110.0 2.2 maximum_dynamic-update-slice_fusion.5
  123.0 2.4 fusion.12
  126.1 2.2 maximum_dynamic-update-slice_fusion.4
  128.3 2.2 maximum_dynamic-update-slice_fusion.5
  141.4 2.4 fusion.12
  144.5 2.2 maximum_dynamic-update-slice_fusion.4
  146.7 2.2 maximum_dynamic-update-slice_fusion.5
  159.7 2.4 fusion.12
  162.8 2.2 maximum_dynamic-update-slice_fusion.4
  165.0 2.2 maximum_dynamic-update-slice_fusion.5
  178.1 2.4 fusion.12
  181.2 2.2 maximum_dynamic-update-slice_fusion.4
  183.4 2.2 maximum_dynamic-update-slice_fusion.5
  188.0 78.1 %pmax.15 = f32[4096]{0:T(1024)S(1)} all-reduce(f32[4096]{0:T(1024)S(1)} %slice.50), channel_id=1, replica_groups=mesh['rows'=32,'cols'=16] {'cols'}, use_global_device_ids=true, to_apply=%region_10.11 | all-reduce | flops 4096 | bytes 32768 | tf_op jit(solution)/shard_map/pmax | solution.py:92
  266.1 3.2 collective-permute-start.1
  269.3 100.7 %all-reduce.4.cloned.1.call-done = f32[65536]{0:T(1024)} async-done(((f32[65536]{0:T(1024)}), f32[65536]{0:T(1024)}) %all-reduce.4.cloned.1.call-update) | async-done | bytes 262160 | tf_op jit(solution)/shard_map/pmax | solution.py:92
  (230 shorter events, 70.5 us)
Async XLA Ops:
  6.5 32.3 %copy-start.3 = (s32[3,64]{1,0:T(4,128)S(1)}, s32[3,64]{1,0:T(4,128)}, u32[]{:S(2)}) copy-start(s32[3,64]{1,0:T(4,128)} %param.5) | copy-start | bytes 2308
  8.2 25.4 %all-to-all-start = ((f32[16,1,4096]{2,1,0:T(1,128)}), f32[16,1,4096]{2,1,0:T(1,128)S(1)}, u32[]{:S(2)}, u32[]{:S(2)}) async-start(f32[16,1,4096]{2,1,0:T(1,128)} %stack.2), calls=%async_computation | async-start | bytes 524288 | tf_op jit(solution)/shard_map/all_to_all | solution.py:64
  22.4 347.6 %all-reduce.4.cloned.1.call-start = ((), (), s32[]{:S(2)}) async-start(), calls=%async_computation.1 | async-start | bytes 524288 | tf_op jit(solution)/shard_map/pmax | solution.py:92
  33.6 4.5 %collective-permute-start = (f32[4096]{0:T(1024)S(1)}, f32[4096]{0:T(1024)S(1)}, u32[]{:S(2)}, u32[]{:S(2)}) collective-permute-start(f32[4096]{0:T(1024)S(1)} %bitcast.19), channel_id=1, source_target_pairs={{16,0},{32,16},{48,32},{64,48},{80,64},{96,80},{112,96},{128,112},... | collective-permute-start | bytes 49160 | tf_op jit(solution)/shard_map/ppermute | solution.py:18
  38.8 4.8 %copy-start.1 = (f32[69632]{0:T(1024)}, f32[69632]{0:T(1024)S(1)}, u32[]{:S(2)}) copy-start(f32[69632]{0:T(1024)S(1)} %get-tuple-element.293) | copy-start | bytes 835588 | tf_op jit(solution)/shard_map/while
  45.5 1.3 copy-start
  48.7 8.5 %copy-start.2 = (f32[69632]{0:T(1024)S(1)}, f32[69632]{0:T(1024)}, u32[]{:S(2)}) copy-start(f32[69632]{0:T(1024)} %copy-done.1) | copy-start | bytes 835588 | tf_op jit(solution)/shard_map/while
  57.2 4.8 %copy-start.1 = (f32[69632]{0:T(1024)}, f32[69632]{0:T(1024)S(1)}, u32[]{:S(2)}) copy-start(f32[69632]{0:T(1024)S(1)} %get-tuple-element.293) | copy-start | bytes 835588 | tf_op jit(solution)/shard_map/while
  63.9 1.3 copy-start
  67.0 8.5 %copy-start.2 = (f32[69632]{0:T(1024)S(1)}, f32[69632]{0:T(1024)}, u32[]{:S(2)}) copy-start(f32[69632]{0:T(1024)} %copy-done.1) | copy-start | bytes 835588 | tf_op jit(solution)/shard_map/while
  75.5 4.8 %copy-start.1 = (f32[69632]{0:T(1024)}, f32[69632]{0:T(1024)S(1)}, u32[]{:S(2)}) copy-start(f32[69632]{0:T(1024)S(1)} %get-tuple-element.293) | copy-start | bytes 835588 | tf_op jit(solution)/shard_map/while
  82.2 1.3 copy-start
  85.4 8.5 %copy-start.2 = (f32[69632]{0:T(1024)S(1)}, f32[69632]{0:T(1024)}, u32[]{:S(2)}) copy-start(f32[69632]{0:T(1024)} %copy-done.1) | copy-start | bytes 835588 | tf_op jit(solution)/shard_map/while
  93.8 4.8 %copy-start.1 = (f32[69632]{0:T(1024)}, f32[69632]{0:T(1024)S(1)}, u32[]{:S(2)}) copy-start(f32[69632]{0:T(1024)S(1)} %get-tuple-element.293) | copy-start | bytes 835588 | tf_op jit(solution)/shard_map/while
  100.5 1.3 copy-start
  103.7 8.5 %copy-start.2 = (f32[69632]{0:T(1024)S(1)}, f32[69632]{0:T(1024)}, u32[]{:S(2)}) copy-start(f32[69632]{0:T(1024)} %copy-done.1) | copy-start | bytes 835588 | tf_op jit(solution)/shard_map/while
  112.2 4.8 %copy-start.1 = (f32[69632]{0:T(1024)}, f32[69632]{0:T(1024)S(1)}, u32[]{:S(2)}) copy-start(f32[69632]{0:T(1024)S(1)} %get-tuple-element.293) | copy-start | bytes 835588 | tf_op jit(solution)/shard_map/while
  118.9 1.3 copy-start
  122.0 8.5 %copy-start.2 = (f32[69632]{0:T(1024)S(1)}, f32[69632]{0:T(1024)}, u32[]{:S(2)}) copy-start(f32[69632]{0:T(1024)} %copy-done.1) | copy-start | bytes 835588 | tf_op jit(solution)/shard_map/while
  130.5 4.8 %copy-start.1 = (f32[69632]{0:T(1024)}, f32[69632]{0:T(1024)S(1)}, u32[]{:S(2)}) copy-start(f32[69632]{0:T(1024)S(1)} %get-tuple-element.293) | copy-start | bytes 835588 | tf_op jit(solution)/shard_map/while
  137.2 1.3 copy-start
  140.4 8.5 %copy-start.2 = (f32[69632]{0:T(1024)S(1)}, f32[69632]{0:T(1024)}, u32[]{:S(2)}) copy-start(f32[69632]{0:T(1024)} %copy-done.1) | copy-start | bytes 835588 | tf_op jit(solution)/shard_map/while
  148.9 4.8 %copy-start.1 = (f32[69632]{0:T(1024)}, f32[69632]{0:T(1024)S(1)}, u32[]{:S(2)}) copy-start(f32[69632]{0:T(1024)S(1)} %get-tuple-element.293) | copy-start | bytes 835588 | tf_op jit(solution)/shard_map/while
  155.6 1.3 copy-start
  158.7 8.5 %copy-start.2 = (f32[69632]{0:T(1024)S(1)}, f32[69632]{0:T(1024)}, u32[]{:S(2)}) copy-start(f32[69632]{0:T(1024)} %copy-done.1) | copy-start | bytes 835588 | tf_op jit(solution)/shard_map/while
  167.2 4.8 %copy-start.1 = (f32[69632]{0:T(1024)}, f32[69632]{0:T(1024)S(1)}, u32[]{:S(2)}) copy-start(f32[69632]{0:T(1024)S(1)} %get-tuple-element.293) | copy-start | bytes 835588 | tf_op jit(solution)/shard_map/while
  173.9 1.3 copy-start
  177.1 8.5 %copy-start.2 = (f32[69632]{0:T(1024)S(1)}, f32[69632]{0:T(1024)}, u32[]{:S(2)}) copy-start(f32[69632]{0:T(1024)} %copy-done.1) | copy-start | bytes 835588 | tf_op jit(solution)/shard_map/while
  266.1 104.9 %collective-permute-start.1 = (f32[4096]{0:T(1024)S(1)}, f32[4096]{0:T(1024)S(1)}, u32[]{:S(2)}, u32[]{:S(2)}) collective-permute-start(f32[4096]{0:T(1024)S(1)} %pmax.15), channel_id=1, source_target_pairs={{0,16},{16,32},{32,48},{48,64},{64,80},{80,96},{96,112},{112,128},... | collective-permute-start | bytes 49160 | tf_op jit(solution)/shard_map/ppermute | solution.py:18
Sparse Core Ops, SparseCore 0:
  187.4 182.5 all-reduce.3
